TPU v7x, 512 devices: a whole 4x4x16 slice. The times are simulated.
512 devices in a mesh: sec: 2 (over z_hi), gx: 16 (over z_lo, core), gy: 16 (over x, y).
Axes of the slice: x: 4, y: 4, z: 16 (z_hi: 2, z_lo: 8; z = z_hi * 8 + z_lo), core: 2. Of those that a mesh axis runs over, the one named last changes fastest.
Arguments:
- terminal: float32 [4, 16, 256, 4096], P('sec', None, 'gx', 'gy'), may hold values from -6 to 6
- forward_temp: bfloat16 [2, 4, 16, 256, 4096], P(None, 'sec', None, 'gx', 'gy'), may hold values from -6 to 6
- conductivity: float32 [16, 256, 4096], P(None, 'gx', 'gy'), may hold values from 0.02 to 0.15
- velocity: float32 [2, 16, 256, 4096], P(None, None, 'gx', 'gy'), may hold values from -0.3 to 0.3
- fixed_mask: int32 [16, 256, 4096], P(None, 'gx', 'gy'), may hold values 0 or 1
- wells: int32 [4, 8, 3], P('sec'), may hold values from 0 to 4095, as said below
- misfit: float32 [2, 4, 8], P(None, 'sec'), may hold values from -12 to 12
- head_gradient: bfloat16 [2, 16, 256, 4096], P('sec', None, 'gx', 'gy'), may hold values from -6 to 6
- blocks: bfloat16 [32, 7, 128, 128], P('gy'), may hold values from -0.1875 to 0.1875
- block_cols: int32 [32, 7], P('gy'), may hold values from 0 to 31, as said below
Outputs:
- head_adjoint: float32 [2, 16, 256, 4096], P('sec', None, 'gx', 'gy')
- sensitivity: float32 [16, 256, 4096], P(None, 'gx', 'gy')
Inputs may be any that keep to these rules, and one draw needn't show every extreme that they name: `wells`: each row is one cell (z, x, y) with z < 16, x < 256, y < 4096; the first test observes the cells (0, 0, 0) and (15, 255, 4095). `block_cols`: row r lists 7 different block columns, the first of which is r.
All inputs are finite; a program needn't handle non-finite values. No bound on the sum of `fixed_mask` on one device may be relied on, other than what follows from the above.
Results may differ from a plain program's by a relative error of at most 0.0029.
Values may be sent and summed in bfloat16 or wider, within the bound.
No kernel may reach another device: no remote copies, remote signals or barrier semaphores. Data moves between devices by JAX's collectives and lax.ppermute only.
A program may use at most 64 MiB of HBM per device.

v0:
```python
import jax
import jax.numpy as jnp
from jax import lax
from jax.sharding import PartitionSpec as P


def extended(cells, sides, width):
    for axis, dim in sides:
        count = lax.axis_size(axis)
        ends = count - 1
        head = lax.slice_in_dim(cells, 0, width, axis=dim)
        tail = lax.slice_in_dim(cells, cells.shape[dim] - width, cells.shape[dim], axis=dim)
        cells = jnp.concatenate(
            [
                lax.ppermute(tail, axis, [(i, (i + 1) % count) for i in range(ends)]),
                cells,
                lax.ppermute(head, axis, [((i + 1) % count, i) for i in range(ends)]),
            ],
            axis=dim,
        )
    return cells


def shifted(padded):
    lead = [(0, 0)] * (padded.ndim - 3)
    deeper = jnp.pad(padded, lead + [(1, 1), (0, 0), (0, 0)])
    centre = deeper[..., 1:-1, 1:-1, 1:-1]
    beside_all = [
        deeper[..., 2:, 1:-1, 1:-1],
        deeper[..., :-2, 1:-1, 1:-1],
        deeper[..., 1:-1, 2:, 1:-1],
        deeper[..., 1:-1, :-2, 1:-1],
        deeper[..., 1:-1, 1:-1, 2:],
        deeper[..., 1:-1, 1:-1, :-2],
    ]
    return (centre, beside_all)


def face_weights(kappa_pad):
    centre, beside_all = shifted(kappa_pad)
    return [
        2.0 * centre * other / jnp.where(centre + other > 0.0, centre + other, 1.0)
        for other in beside_all
    ]


def advance(adjoint_pad, weights, keep, speed_x, speed_y, source):
    centre, beside_all = shifted(adjoint_pad)
    diffusion = weights[0] * (beside_all[0] - centre)
    for face in range(1, 6):
        diffusion = diffusion + weights[face] * (beside_all[face] - centre)
    slope_x = 0.5 * (beside_all[2] - beside_all[3])
    slope_y = 0.5 * (beside_all[4] - beside_all[5])
    updated = keep * (centre + diffusion + speed_x * slope_x + speed_y * slope_y + source)
    return (updated, diffusion, slope_x, slope_y)


def well_sources(wells, misfit_level, layers, rows_x, cols_y, margin):
    start_x = lax.axis_index("gx") * rows_x - margin
    start_y = lax.axis_index("gy") * cols_y - margin
    coord_z = jnp.arange(layers, dtype=jnp.int32)[:, None, None]
    coord_x = (start_x + jnp.arange(rows_x + 2 * margin, dtype=jnp.int32))[None, :, None]
    coord_y = (start_y + jnp.arange(cols_y + 2 * margin, dtype=jnp.int32))[None, None, :]
    well_z = wells[:, :, 0][:, :, None, None, None]
    well_x = wells[:, :, 1][:, :, None, None, None]
    well_y = wells[:, :, 2][:, :, None, None, None]
    matches = (coord_z == well_z) & (coord_x == well_x) & (coord_y == well_y)
    return jnp.sum(jnp.where(matches, misfit_level[:, :, None, None, None], 0.0), axis=1)


def shards(
    terminal,
    forward_temp,
    conductivity,
    velocity,
    fixed_mask,
    wells,
    misfit,
    head_gradient,
    blocks,
    block_cols,
):
    layers, rows_x, cols_y = conductivity.shape
    steps = forward_temp.shape[0]
    keep = 1.0 - fixed_mask.astype(jnp.float32)
    heat_sens = jnp.zeros((layers, rows_x, cols_y), jnp.float32)
    flow_x = jnp.zeros((layers, rows_x, cols_y), jnp.float32)
    flow_y = jnp.zeros((layers, rows_x, cols_y), jnp.float32)
    kappa_pad = extended(conductivity, (("gx", 1), ("gy", 2)), 1)
    weights = face_weights(kappa_pad)
    adjoint = terminal
    for level in reversed(range(steps)):
        padded = extended(adjoint, (("gx", 2), ("gy", 3)), 1)
        source = well_sources(wells, misfit[level], layers, rows_x, cols_y, 0)
        adjoint, diffusion, slope_x, slope_y = advance(
            padded, weights, keep, velocity[0], velocity[1], source
        )
        temper = forward_temp[level].astype(jnp.float32)
        heat_sens = heat_sens + jnp.sum(temper * diffusion, axis=0)
        flow_x = flow_x + jnp.sum(temper * slope_x, axis=0)
        flow_y = flow_y + jnp.sum(temper * slope_y, axis=0)
    summed = lax.psum_scatter(jnp.stack([flow_x, flow_y]), "sec", scatter_dimension=0, tiled=True)
    rounded = summed[0].astype(jnp.bfloat16)
    row_blocks, per_row, block_size, _ = blocks.shape
    piece = lax.all_gather(rounded, "gy", axis=2, tiled=True)
    count = piece.shape[2] // block_size
    split_rows = piece.reshape(layers, rows_x, count, block_size)
    block_ids = jnp.arange(count, dtype=jnp.int32)
    chosen = (block_cols[:, :, None] == block_ids[None, None, :]).astype(jnp.bfloat16)
    portion = jnp.einsum("bkq,zxqj->bkzxj", chosen, split_rows, preferred_element_type=jnp.float32)
    picked = portion.astype(jnp.bfloat16)
    head = jnp.einsum(
        "bkzxj,bkij->zxbi", picked, blocks, preferred_element_type=jnp.float32
    ).reshape(layers, rows_x, cols_y)
    partial_sens = heat_sens + head * head_gradient[0].astype(jnp.float32)
    sensitivity = lax.psum(partial_sens, "sec")
    return (head[None], sensitivity)


def solution(mesh):
    placed = (
        P("sec", None, "gx", "gy"),
        P(None, "sec", None, "gx", "gy"),
        P(None, "gx", "gy"),
        P(None, None, "gx", "gy"),
        P(None, "gx", "gy"),
        P("sec", None, None),
        P(None, "sec", None),
        P("sec", None, "gx", "gy"),
        P("gy", None, None, None),
        P("gy", None),
    )
    return jax.shard_map(
        shards,
        mesh=mesh,
        in_specs=placed,
        out_specs=(P("sec", None, "gx", "gy"), P(None, "gx", "gy")),
        check_vma=False,
    )
```

profile of v0, /device:TPU:1, one launch (start us, length us, event | category | flops | bytes accessed | tf_op | source)
XLA Modules:
  0.0 278.9 jit_solution(739867863807899032)
XLA Ops:
  8.3 4.9 %collective-permute-start.2 = (f32[16,1,256]{2,1,0:T(1,128)S(1)}, f32[16,1,256]{2,1,0:T(1,128)S(1)}, u32[]{:S(2)}, u32[]{:S(2)}) collective-permute-start(f32[16,1,256]{2,1,0:T(1,128)S(1)} %get-tuple-element.29), channel_id=1, source_target_pairs={{0,16},{16,32},{32,48},{48,64},{64,80},{80,96},{96,112},{112,128},... | collective-permute-start | bytes 49160 | tf_op jit(solution)/shard_map/ppermute | solution.py:15
  13.3 5.1 %collective-permute-start.3 = (f32[16,1,256]{2,1,0:T(1,128)S(1)}, f32[16,1,256]{2,1,0:T(1,128)S(1)}, u32[]{:S(2)}, u32[]{:S(2)}) collective-permute-start(f32[16,1,256]{2,1,0:T(1,128)S(1)} %get-tuple-element.30), channel_id=1, source_target_pairs={{16,0},{32,16},{48,32},{64,48},{80,64},{96,80},{112,96},{128,112},... | collective-permute-start | bytes 49160 | tf_op jit(solution)/shard_map/ppermute | solution.py:17
  19.5 1.9 collective-permute-start
  21.4 3.6 %collective-permute-start.1 = (f32[2,16,1,256]{3,2,1,0:T(1,128)S(1)}, f32[2,16,1,256]{3,2,1,0:T(1,128)S(1)}, u32[]{:S(2)}, u32[]{:S(2)}) collective-permute-start(f32[2,16,1,256]{3,2,1,0:T(1,128)S(1)} %get-tuple-element.20), channel_id=1, source_target_pairs={{0,16},{16,32},{32,48},{48,64},{64,80},{80,96},{96,112},{112,128},... | collective-permute-start | bytes 98312 | tf_op jit(solution)/shard_map/ppermute | solution.py:15
  27.5 1.4 collective-permute-start.4
  28.9 1.3 collective-permute-start.5
  31.1 1.5 collective-permute-done.4
  32.6 4.1 %collective-permute-done.5 = f32[16,18,1]{2,1,0:T(8,128)S(1)} collective-permute-done((f32[16,18,1]{2,1,0:T(8,128)S(1)}, f32[16,18,1]{2,1,0:T(8,128)S(1)}, u32[]{:S(2)}, u32[]{:S(2)}) %collective-permute-start.5) | collective-permute-done | bytes 1184 | tf_op jit(solution)/shard_map/ppermute | solution.py:17
  37.4 2.2 collective-permute-start.6
  41.5 6.3 %collective-permute-done.6 = f32[2,16,18,1]{3,2,1,0:T(8,128)S(1)} collective-permute-done((f32[2,16,18,1]{3,2,1,0:T(8,128)S(1)}, f32[2,16,18,1]{3,2,1,0:T(8,128)S(1)}, u32[]{:S(2)}, u32[]{:S(2)}) %collective-permute-start.6) | collective-permute-done | bytes 2336 | tf_op jit(solution)/shard_map/ppermute | solution.py:15
  47.8 3.8 %collective-permute-done.7 = f32[2,16,18,1]{3,2,1,0:T(8,128)S(1)} collective-permute-done((f32[2,16,18,1]{3,2,1,0:T(8,128)S(1)}, f32[2,16,18,1]{3,2,1,0:T(8,128)S(1)}, u32[]{:S(2)}, u32[]{:S(2)}) %collective-permute-start.7) | collective-permute-done | bytes 2336 | tf_op jit(solution)/shard_map/ppermute | solution.py:17
  53.5 3.3 %collective-permute-start.8 = (f32[2,16,1,256]{3,2,1,0:T(1,128)S(1)}, f32[2,16,1,256]{3,2,1,0:T(1,128)S(1)}, u32[]{:S(2)}, u32[]{:S(2)}) collective-permute-start(f32[2,16,1,256]{3,2,1,0:T(1,128)S(1)} %get-tuple-element.15), channel_id=1, source_target_pairs={{16,0},{32,16},{48,32},{64,48},{80,64},{96,80},{112,96},{128,112},... | collective-permute-start | bytes 98312 | tf_op jit(solution)/shard_map/ppermute | solution.py:17
  56.8 3.8 %collective-permute-start.9 = (f32[2,16,1,256]{3,2,1,0:T(1,128)S(1)}, f32[2,16,1,256]{3,2,1,0:T(1,128)S(1)}, u32[]{:S(2)}, u32[]{:S(2)}) collective-permute-start(f32[2,16,1,256]{3,2,1,0:T(1,128)S(1)} %get-tuple-element.16), channel_id=1, source_target_pairs={{0,16},{16,32},{32,48},{48,64},{64,80},{80,96},{96,112},{112,128},... | collective-permute-start | bytes 98312 | tf_op jit(solution)/shard_map/ppermute | solution.py:15
  63.2 5.1 %collective-permute-start.11 = (f32[2,16,18,1]{3,2,1,0:T(8,128)S(1)}, f32[2,16,18,1]{3,2,1,0:T(8,128)S(1)}, u32[]{:S(2)}, u32[]{:S(2)}) collective-permute-start(f32[2,16,18,1]{3,2,1,0:T(8,128)S(1)} %get-tuple-element.12), channel_id=1, source_target_pairs={{0,1},{1,2},{2,3},{3,4},{4,5},{5,6},{6,7},{7,8},{8,9},{9,10},{10,1... | collective-permute-start | bytes 6920 | tf_op jit(solution)/shard_map/ppermute | solution.py:15
  68.9 5.6 %collective-permute-done.10 = f32[2,16,18,1]{3,2,1,0:T(8,128)S(1)} collective-permute-done((f32[2,16,18,1]{3,2,1,0:T(8,128)S(1)}, f32[2,16,18,1]{3,2,1,0:T(8,128)S(1)}, u32[]{:S(2)}, u32[]{:S(2)}) %collective-permute-start.10) | collective-permute-done | bytes 2336 | tf_op jit(solution)/shard_map/ppermute | solution.py:17
  74.5 1.8 collective-permute-done.11
  76.2 1.3 fusion.7
  78.5 59.7 %reduce-scatter.2.cloned.1.call-done = f32[1,16,16,256]{3,2,1,0:T(8,128)} async-done(((f32[2,16,16,256]{3,2,1,0:T(8,128)}), f32[1,16,16,256]{3,2,1,0:T(8,128)}) %reduce-scatter.2.cloned.1.call-update) | async-done | bytes 262160 | tf_op jit(solution)/shard_map/reduce_scatter | solution.py:102
  138.3 1.6 convert_element_type.41
  141.0 1.7 fusion.9
  142.7 52.4 %all-gather.3.cloned.1.call-done = bf16[1,16,16,4096]{3,2,1,0:T(8,128)(2,1)} async-done(((bf16[1,16,16,256]{3,2,1,0:T(8,128)(2,1)}), bf16[1,16,16,4096]{3,2,1,0:T(8,128)(2,1)}) %all-gather.3.cloned.1.call-update) | async-done | bytes 2097168 | tf_op jit(solution)/shard_map/all_gather | solution.py:105
  195.1 2.1 copy.21
  200.7 70.0 %all-reduce.5.cloned.1.call-done = f32[16,16,256]{2,1,0:T(8,128)} async-done(((f32[16,16,256]{2,1,0:T(8,128)}), f32[16,16,256]{2,1,0:T(8,128)}) %all-reduce.5.cloned.1.call-update) | async-done | bytes 262160 | tf_op jit(solution)/shard_map/psum | solution.py:116
  270.7 1.7 copy.26
  (69 shorter events, 18.4 us)
Async XLA Ops:
  7.2 190.6 %copy-start = (bf16[2,7,128,128]{3,2,1,0:T(8,128)(2,1)S(1)}, bf16[2,7,128,128]{3,2,1,0:T(8,128)(2,1)}, u32[]{:S(2)}) copy-start(bf16[2,7,128,128]{3,2,1,0:T(8,128)(2,1)} %param.18) | copy-start | bytes 1376260
  7.2 20.1 %copy-start.2 = (f32[16,16,256]{2,1,0:T(8,128)S(1)}, f32[16,16,256]{2,1,0:T(8,128)}, u32[]{:S(2)}) copy-start(f32[16,16,256]{2,1,0:T(8,128)} %param.12) | copy-start | bytes 786436
  7.2 19.8 %copy-start.7 = (s32[16,16,256]{2,1,0:T(8,128)S(1)}, s32[16,16,256]{2,1,0:T(8,128)}, u32[]{:S(2)}) copy-start(s32[16,16,256]{2,1,0:T(8,128)} %param.14) | copy-start | bytes 786436
  7.2 20.1 %copy-start.10 = (f32[2,2,8]{2,1,0:T(2,128)S(1)}, f32[2,2,8]{2,1,0:T(2,128)}, u32[]{:S(2)}) copy-start(f32[2,2,8]{2,1,0:T(2,128)} %param.16) | copy-start | bytes 388
  7.2 131.1 %reduce-scatter.2.cloned.1.call-start = ((), (), s32[]{:S(2)}) async-start(), calls=%async_computation.1 | async-start | bytes 786432 | tf_op jit(solution)/shard_map/reduce_scatter | solution.py:102
  8.3 18.9 %collective-permute-start.2 = (f32[16,1,256]{2,1,0:T(1,128)S(1)}, f32[16,1,256]{2,1,0:T(1,128)S(1)}, u32[]{:S(2)}, u32[]{:S(2)}) collective-permute-start(f32[16,1,256]{2,1,0:T(1,128)S(1)} %get-tuple-element.29), channel_id=1, source_target_pairs={{0,16},{16,32},{32,48},{48,64},{64,80},{80,96},{96,112},{112,128},... | collective-permute-start | bytes 49160 | tf_op jit(solution)/shard_map/ppermute | solution.py:15
  13.3 14.0 %collective-permute-start.3 = (f32[16,1,256]{2,1,0:T(1,128)S(1)}, f32[16,1,256]{2,1,0:T(1,128)S(1)}, u32[]{:S(2)}, u32[]{:S(2)}) collective-permute-start(f32[16,1,256]{2,1,0:T(1,128)S(1)} %get-tuple-element.30), channel_id=1, source_target_pairs={{16,0},{32,16},{48,32},{64,48},{80,64},{96,80},{112,96},{128,112},... | collective-permute-start | bytes 49160 | tf_op jit(solution)/shard_map/ppermute | solution.py:17
  19.5 17.6 %collective-permute-start = (f32[2,16,1,256]{3,2,1,0:T(1,128)S(1)}, f32[2,16,1,256]{3,2,1,0:T(1,128)S(1)}, u32[]{:S(2)}, u32[]{:S(2)}) collective-permute-start(f32[2,16,1,256]{3,2,1,0:T(1,128)S(1)} %get-tuple-element.19), channel_id=1, source_target_pairs={{16,0},{32,16},{48,32},{64,48},{80,64},{96,80},{112,96},{128,112},... | collective-permute-start | bytes 98312 | tf_op jit(solution)/shard_map/ppermute | solution.py:17
  21.4 15.7 %collective-permute-start.1 = (f32[2,16,1,256]{3,2,1,0:T(1,128)S(1)}, f32[2,16,1,256]{3,2,1,0:T(1,128)S(1)}, u32[]{:S(2)}, u32[]{:S(2)}) collective-permute-start(f32[2,16,1,256]{3,2,1,0:T(1,128)S(1)} %get-tuple-element.20), channel_id=1, source_target_pairs={{0,16},{16,32},{32,48},{48,64},{64,80},{80,96},{96,112},{112,128},... | collective-permute-start | bytes 98312 | tf_op jit(solution)/shard_map/ppermute | solution.py:15
  27.4 9.7 %copy-start.1 = (f32[2,16,16,256]{3,2,1,0:T(8,128)S(1)}, f32[2,16,16,256]{3,2,1,0:T(8,128)}, u32[]{:S(2)}) copy-start(f32[2,16,16,256]{3,2,1,0:T(8,128)} %param.10) | copy-start | bytes 1572868
  27.5 5.1 %collective-permute-start.4 = (f32[16,18,1]{2,1,0:T(8,128)S(1)}, f32[16,18,1]{2,1,0:T(8,128)S(1)}, u32[]{:S(2)}, u32[]{:S(2)}) collective-permute-start(f32[16,18,1]{2,1,0:T(8,128)S(1)} %get-tuple-element.22), channel_id=1, source_target_pairs={{0,1},{1,2},{2,3},{3,4},{4,5},{5,6},{6,7},{7,8},{8,9},{9,10},{10,1... | collective-permute-start | bytes 3464 | tf_op jit(solution)/shard_map/ppermute | solution.py:15
  28.9 7.8 %collective-permute-start.5 = (f32[16,18,1]{2,1,0:T(8,128)S(1)}, f32[16,18,1]{2,1,0:T(8,128)S(1)}, u32[]{:S(2)}, u32[]{:S(2)}) collective-permute-start(f32[16,18,1]{2,1,0:T(8,128)S(1)} %get-tuple-element.21), channel_id=1, source_target_pairs={{1,0},{2,1},{3,2},{4,3},{5,4},{6,5},{7,6},{8,7},{9,8},{10,9},{11,1... | collective-permute-start | bytes 3464 | tf_op jit(solution)/shard_map/ppermute | solution.py:17
  37.4 10.4 %collective-permute-start.6 = (f32[2,16,18,1]{3,2,1,0:T(8,128)S(1)}, f32[2,16,18,1]{3,2,1,0:T(8,128)S(1)}, u32[]{:S(2)}, u32[]{:S(2)}) collective-permute-start(f32[2,16,18,1]{3,2,1,0:T(8,128)S(1)} %get-tuple-element.14), channel_id=1, source_target_pairs={{0,1},{1,2},{2,3},{3,4},{4,5},{5,6},{6,7},{7,8},{8,9},{9,10},{10,1... | collective-permute-start | bytes 6920 | tf_op jit(solution)/shard_map/ppermute | solution.py:15
  39.6 12.0 %collective-permute-start.7 = (f32[2,16,18,1]{3,2,1,0:T(8,128)S(1)}, f32[2,16,18,1]{3,2,1,0:T(8,128)S(1)}, u32[]{:S(2)}, u32[]{:S(2)}) collective-permute-start(f32[2,16,18,1]{3,2,1,0:T(8,128)S(1)} %get-tuple-element.13), channel_id=1, source_target_pairs={{1,0},{2,1},{3,2},{4,3},{5,4},{6,5},{7,6},{8,7},{9,8},{10,9},{11,1... | collective-permute-start | bytes 6920 | tf_op jit(solution)/shard_map/ppermute | solution.py:17
  53.5 7.1 %collective-permute-start.8 = (f32[2,16,1,256]{3,2,1,0:T(1,128)S(1)}, f32[2,16,1,256]{3,2,1,0:T(1,128)S(1)}, u32[]{:S(2)}, u32[]{:S(2)}) collective-permute-start(f32[2,16,1,256]{3,2,1,0:T(1,128)S(1)} %get-tuple-element.15), channel_id=1, source_target_pairs={{16,0},{32,16},{48,32},{64,48},{80,64},{96,80},{112,96},{128,112},... | collective-permute-start | bytes 98312 | tf_op jit(solution)/shard_map/ppermute | solution.py:17
  56.8 11.5 %copy-start.3 = (bf16[2,2,16,16,256]{4,3,2,1,0:T(8,128)(2,1)S(1)}, bf16[2,2,16,16,256]{4,3,2,1,0:T(8,128)(2,1)}, u32[]{:S(2)}) copy-start(bf16[2,2,16,16,256]{4,3,2,1,0:T(8,128)(2,1)} %param.11) | copy-start | bytes 1572868
  56.8 4.8 %collective-permute-start.9 = (f32[2,16,1,256]{3,2,1,0:T(1,128)S(1)}, f32[2,16,1,256]{3,2,1,0:T(1,128)S(1)}, u32[]{:S(2)}, u32[]{:S(2)}) collective-permute-start(f32[2,16,1,256]{3,2,1,0:T(1,128)S(1)} %get-tuple-element.16), channel_id=1, source_target_pairs={{0,16},{16,32},{32,48},{48,64},{64,80},{80,96},{96,112},{112,128},... | collective-permute-start | bytes 98312 | tf_op jit(solution)/shard_map/ppermute | solution.py:15
  61.9 12.6 %collective-permute-start.10 = (f32[2,16,18,1]{3,2,1,0:T(8,128)S(1)}, f32[2,16,18,1]{3,2,1,0:T(8,128)S(1)}, u32[]{:S(2)}, u32[]{:S(2)}) collective-permute-start(f32[2,16,18,1]{3,2,1,0:T(8,128)S(1)} %get-tuple-element.11), channel_id=1, source_target_pairs={{1,0},{2,1},{3,2},{4,3},{5,4},{6,5},{7,6},{8,7},{9,8},{10,9},{11,1... | collective-permute-start | bytes 6920 | tf_op jit(solution)/shard_map/ppermute | solution.py:17
  63.2 13.0 %collective-permute-start.11 = (f32[2,16,18,1]{3,2,1,0:T(8,128)S(1)}, f32[2,16,18,1]{3,2,1,0:T(8,128)S(1)}, u32[]{:S(2)}, u32[]{:S(2)}) collective-permute-start(f32[2,16,18,1]{3,2,1,0:T(8,128)S(1)} %get-tuple-element.12), channel_id=1, source_target_pairs={{0,1},{1,2},{2,3},{3,4},{4,5},{5,6},{6,7},{7,8},{8,9},{9,10},{10,1... | collective-permute-start | bytes 6920 | tf_op jit(solution)/shard_map/ppermute | solution.py:15
  78.5 116.6 %all-gather.3.cloned.1.call-start = ((), (), s32[]{:S(2)}) async-start(), calls=%async_computation.3 | async-start | bytes 2228224 | tf_op jit(solution)/shard_map/all_gather | solution.py:105
  139.9 130.8 %all-reduce.5.cloned.1.call-start = ((), (), s32[]{:S(2)}) async-start(), calls=%async_computation.2 | async-start | bytes 524288 | tf_op jit(solution)/shard_map/psum | solution.py:116
  140.0 1.0 copy-start.4
  195.1 2.1 copy-start.9
  197.8 1.0 copy-start.8
  (2 other events, 2.0 us)
Sparse Core Ops, SparseCore 0:
  78.6 59.6 reduce-scatter.1
  141.7 53.3 all-gather.2
  199.7 70.9 all-reduce.4
where the time goes:
time: 280 us; the launch traced here: 279 us
  waiting for transfers between devices  206 us (74%)
  starting transfers between devices  35.4 us (13%)
  between operations  14.1 us (5%)
  other arithmetic  12.9 us (5%)
  local copies, waits for them, and re-layouts  9.19 us (3%)
    psum x1, waiting for transfers between devices, shards(): sensitivity = lax.psum(partial_sens, 'sec')  70 us
    reduce_scatter x1, waiting for transfers between devices, shards(): lax.psum_scatter(jnp.stack([flow_x, flow_y]), 'sec', scatter_dimension=0,...  59.7 us
    all_gather x1, waiting for transfers between devices, shards(): piece = lax.all_gather(rounded, 'gy', axis=2, tiled=True)  52.4 us
    ppermute x6, starting transfers between devices, extended(): lax.ppermute(tail, axis, [(i, (i + 1) % count) for i in range(ends)])  21 us
    ppermute x6, starting transfers between devices, extended(): lax.ppermute(head, axis, [((i + 1) % count, i) for i in range(ends)])  14.3 us
    ppermute x6, waiting for transfers between devices, extended(): lax.ppermute(head, axis, [((i + 1) % count, i) for i in range(ends)])  13.5 us
    ppermute x6, waiting for transfers between devices, extended(): lax.ppermute(tail, axis, [(i, (i + 1) % count) for i in range(ends)])  10.6 us
  transfers between devices with their start and end apart: 15, of which 10 were waited for; matrix products, arithmetic and copies ran while one was open for 3% of the time, Pallas kernels for 0%

commit v1 on v0

--- a/solution.py
+++ b/solution.py
@@ -2,6 +2,22 @@
 import jax.numpy as jnp
 from jax import lax
 from jax.sharding import PartitionSpec as P
+
+
+def gather_around(x, axis, dim):
+    ways, here, step = (lax.axis_size(axis), lax.axis_index(axis), x.shape[dim])
+    shape = [n * ways if d == dim else n for d, n in enumerate(x.shape)]
+    full = lax.dynamic_update_slice_in_dim(jnp.zeros(shape, x.dtype), x, here * step, axis=dim)
+    going_up = going_down = x
+    for far in range(1, ways // 2 + 1):
+        going_up = lax.ppermute(going_up, axis, [(d, (d + 1) % ways) for d in range(ways)])
+        full = lax.dynamic_update_slice_in_dim(full, going_up, (here - far) % ways * step, axis=dim)
+        if 2 * far < ways:
+            going_down = lax.ppermute(going_down, axis, [(d, (d - 1) % ways) for d in range(ways)])
+            full = lax.dynamic_update_slice_in_dim(
+                full, going_down, (here + far) % ways * step, axis=dim
+            )
+    return full
 
 
 def extended(cells, sides, width):
@@ -102,7 +118,7 @@
     summed = lax.psum_scatter(jnp.stack([flow_x, flow_y]), "sec", scatter_dimension=0, tiled=True)
     rounded = summed[0].astype(jnp.bfloat16)
     row_blocks, per_row, block_size, _ = blocks.shape
-    piece = lax.all_gather(rounded, "gy", axis=2, tiled=True)
+    piece = gather_around(rounded, "gy", 2)
     count = piece.shape[2] // block_size
     split_rows = piece.reshape(layers, rows_x, count, block_size)
     block_ids = jnp.arange(count, dtype=jnp.int32)

time: 280 us -> 293 us (1.046)
  starting transfers between devices: 35.4 us -> 97.3 us
  waiting for transfers between devices: 206 us -> 157 us
    ppermute x0 -> x15, starting transfers between devices: none -> 62.1 us  [the longest x7 45.6 us: gather_around(): lax.ppermute(going_down, axis, [(d, (d - 1) % ways) for d in range(ways)])]
    all_gather x1 -> x0, waiting for transfers between devices: 52.4 us -> none  [shards(): piece = lax.all_gather(rounded, 'gy', axis=2, tiled=True)]
    ppermute x0 -> x15, waiting for transfers between devices: none -> 9.28 us  [the longest x8 9.26 us: gather_around(): lax.ppermute(going_up, axis, [(d, (d + 1) % ways) for d in range(ways)])]
    psum x1, waiting for transfers between devices: 70 us -> 65 us  [shards(): sensitivity = lax.psum(partial_sens, 'sec')]
  transfers between devices with their start and end apart: 15 -> 29, of which waited for: 10 -> 16; matrix products, arithmetic and copies ran while one was open for 3% -> 4% of each run, Pallas kernels for 0% -> 0%
where the time goes in v1:
time: 293 us; the launch traced here: 292 us
  waiting for transfers between devices  157 us (54%)
  starting transfers between devices  97.3 us (33%)
  between operations  15.1 us (5%)
  other arithmetic  12.6 us (4%)
  local copies, waits for them, and re-layouts  8.77 us (3%)
    psum x1, waiting for transfers between devices, shards(): sensitivity = lax.psum(partial_sens, 'sec')  65 us
    reduce_scatter x1, waiting for transfers between devices, shards(): lax.psum_scatter(jnp.stack([flow_x, flow_y]), 'sec', scatter_dimension=0,...  58.7 us
    ppermute x7, starting transfers between devices, gather_around(): lax.ppermute(going_down, axis, [(d, (d - 1) % ways) for d in range(ways)])  45.6 us
    ppermute x6, starting transfers between devices, extended(): lax.ppermute(tail, axis, [(i, (i + 1) % count) for i in range(ends)])  20.8 us
    ppermute x8, starting transfers between devices, gather_around(): lax.ppermute(going_up, axis, [(d, (d + 1) % ways) for d in range(ways)])  16.5 us
    ppermute x6, starting transfers between devices, extended(): lax.ppermute(head, axis, [((i + 1) % count, i) for i in range(ends)])  14.4 us
    ppermute x6, waiting for transfers between devices, extended(): lax.ppermute(head, axis, [((i + 1) % count, i) for i in range(ends)])  13.5 us
    ppermute x6, waiting for transfers between devices, extended(): lax.ppermute(tail, axis, [(i, (i + 1) % count) for i in range(ends)])  10.5 us
  transfers between devices with their start and end apart: 29, of which 16 were waited for; matrix products, arithmetic and copies ran while one was open for 4% of the time, Pallas kernels for 0%

profile of v1, /device:TPU:1, one launch (start us, length us, event | category | flops | bytes accessed | tf_op | source)
XLA Modules:
  0.0 291.7 jit_solution(5343175929800406602)
XLA Ops:
  8.3 4.9 %collective-permute-start.2 = (f32[16,1,256]{2,1,0:T(1,128)S(1)}, f32[16,1,256]{2,1,0:T(1,128)S(1)}, u32[]{:S(2)}, u32[]{:S(2)}) collective-permute-start(f32[16,1,256]{2,1,0:T(1,128)S(1)} %get-tuple-element.31), channel_id=1, source_target_pairs={{0,16},{16,32},{32,48},{48,64},{64,80},{80,96},{96,112},{112,128},... | collective-permute-start | bytes 49160 | tf_op jit(solution)/shard_map/ppermute | solution.py:31
  13.2 5.1 %collective-permute-start.3 = (f32[16,1,256]{2,1,0:T(1,128)S(1)}, f32[16,1,256]{2,1,0:T(1,128)S(1)}, u32[]{:S(2)}, u32[]{:S(2)}) collective-permute-start(f32[16,1,256]{2,1,0:T(1,128)S(1)} %get-tuple-element.32), channel_id=1, source_target_pairs={{16,0},{32,16},{48,32},{64,48},{80,64},{96,80},{112,96},{128,112},... | collective-permute-start | bytes 49160 | tf_op jit(solution)/shard_map/ppermute | solution.py:33
  19.5 1.9 collective-permute-start
  21.4 3.6 %collective-permute-start.1 = (f32[2,16,1,256]{3,2,1,0:T(1,128)S(1)}, f32[2,16,1,256]{3,2,1,0:T(1,128)S(1)}, u32[]{:S(2)}, u32[]{:S(2)}) collective-permute-start(f32[2,16,1,256]{3,2,1,0:T(1,128)S(1)} %get-tuple-element.22), channel_id=1, source_target_pairs={{0,16},{16,32},{32,48},{48,64},{64,80},{80,96},{96,112},{112,128},... | collective-permute-start | bytes 98312 | tf_op jit(solution)/shard_map/ppermute | solution.py:31
  35.0 4.1 %collective-permute-done.5 = f32[16,18,1]{2,1,0:T(8,128)S(1)} collective-permute-done((f32[16,18,1]{2,1,0:T(8,128)S(1)}, f32[16,18,1]{2,1,0:T(8,128)S(1)}, u32[]{:S(2)}, u32[]{:S(2)}) %collective-permute-start.5) | collective-permute-done | bytes 1184 | tf_op jit(solution)/shard_map/ppermute | solution.py:33
  39.9 2.2 collective-permute-start.6
  44.0 6.3 %collective-permute-done.6 = f32[2,16,18,1]{3,2,1,0:T(8,128)S(1)} collective-permute-done((f32[2,16,18,1]{3,2,1,0:T(8,128)S(1)}, f32[2,16,18,1]{3,2,1,0:T(8,128)S(1)}, u32[]{:S(2)}, u32[]{:S(2)}) %collective-permute-start.6) | collective-permute-done | bytes 2336 | tf_op jit(solution)/shard_map/ppermute | solution.py:31
  50.2 3.8 %collective-permute-done.7 = f32[2,16,18,1]{3,2,1,0:T(8,128)S(1)} collective-permute-done((f32[2,16,18,1]{3,2,1,0:T(8,128)S(1)}, f32[2,16,18,1]{3,2,1,0:T(8,128)S(1)}, u32[]{:S(2)}, u32[]{:S(2)}) %collective-permute-start.7) | collective-permute-done | bytes 2336 | tf_op jit(solution)/shard_map/ppermute | solution.py:33
  56.0 3.5 %collective-permute-start.8 = (f32[2,16,1,256]{3,2,1,0:T(1,128)S(1)}, f32[2,16,1,256]{3,2,1,0:T(1,128)S(1)}, u32[]{:S(2)}, u32[]{:S(2)}) collective-permute-start(f32[2,16,1,256]{3,2,1,0:T(1,128)S(1)} %get-tuple-element.17), channel_id=1, source_target_pairs={{16,0},{32,16},{48,32},{64,48},{80,64},{96,80},{112,96},{128,112},... | collective-permute-start | bytes 98312 | tf_op jit(solution)/shard_map/ppermute | solution.py:33
  59.4 3.7 %collective-permute-start.9 = (f32[2,16,1,256]{3,2,1,0:T(1,128)S(1)}, f32[2,16,1,256]{3,2,1,0:T(1,128)S(1)}, u32[]{:S(2)}, u32[]{:S(2)}) collective-permute-start(f32[2,16,1,256]{3,2,1,0:T(1,128)S(1)} %get-tuple-element.18), channel_id=1, source_target_pairs={{0,16},{16,32},{32,48},{48,64},{64,80},{80,96},{96,112},{112,128},... | collective-permute-start | bytes 98312 | tf_op jit(solution)/shard_map/ppermute | solution.py:31
  65.7 5.1 %collective-permute-start.11 = (f32[2,16,18,1]{3,2,1,0:T(8,128)S(1)}, f32[2,16,18,1]{3,2,1,0:T(8,128)S(1)}, u32[]{:S(2)}, u32[]{:S(2)}) collective-permute-start(f32[2,16,18,1]{3,2,1,0:T(8,128)S(1)} %get-tuple-element.14), channel_id=1, source_target_pairs={{0,1},{1,2},{2,3},{3,4},{4,5},{5,6},{6,7},{7,8},{8,9},{9,10},{10,1... | collective-permute-start | bytes 6920 | tf_op jit(solution)/shard_map/ppermute | solution.py:31
  71.4 5.6 %collective-permute-done.10 = f32[2,16,18,1]{3,2,1,0:T(8,128)S(1)} collective-permute-done((f32[2,16,18,1]{3,2,1,0:T(8,128)S(1)}, f32[2,16,18,1]{3,2,1,0:T(8,128)S(1)}, u32[]{:S(2)}, u32[]{:S(2)}) %collective-permute-start.10) | collective-permute-done | bytes 2336 | tf_op jit(solution)/shard_map/ppermute | solution.py:33
  82.0 58.7 %reduce-scatter.2.cloned.1.call-done = f32[1,16,16,256]{3,2,1,0:T(8,128)} async-done(((f32[2,16,16,256]{3,2,1,0:T(8,128)}), f32[1,16,16,256]{3,2,1,0:T(8,128)}) %reduce-scatter.2.cloned.1.call-update) | async-done | bytes 262160 | tf_op jit(solution)/shard_map/reduce_scatter | solution.py:118
  141.7 3.1 %collective-permute-start.12 = (bf16[16,16,256]{2,1,0:T(8,128)(2,1)S(1)}, bf16[16,16,256]{2,1,0:T(8,128)(2,1)S(1)}, u32[]{:S(2)}, u32[]{:S(2)}) collective-permute-start(bf16[16,16,256]{2,1,0:T(8,128)(2,1)S(1)} %get-tuple-element.8), channel_id=1, source_target_pairs={{0,1},{1,2},{2,3},{3,4},{4,5},{5,6},{6,7},{7,8},{8,9},{9,10},{10,1... | collective-permute-start | bytes 393224 | tf_op jit(solution)/shard_map/ppermute | solution.py:13
  144.8 5.5 %collective-permute-start.13 = (bf16[16,16,256]{2,1,0:T(8,128)(2,1)S(1)}, bf16[16,16,256]{2,1,0:T(8,128)(2,1)S(1)}, u32[]{:S(2)}, u32[]{:S(2)}) collective-permute-start(bf16[16,16,256]{2,1,0:T(8,128)(2,1)S(1)} %get-tuple-element.8), channel_id=1, source_target_pairs={{0,15},{1,0},{2,1},{3,2},{4,3},{5,4},{6,5},{7,6},{8,7},{9,8},{10,9... | collective-permute-start | bytes 393224 | tf_op jit(solution)/shard_map/ppermute | solution.py:16
  153.3 6.7 %collective-permute-start.15 = (bf16[16,16,256]{2,1,0:T(8,128)(2,1)S(1)}, bf16[16,16,256]{2,1,0:T(8,128)(2,1)S(1)}, u32[]{:S(2)}, u32[]{:S(2)}) collective-permute-start(bf16[16,16,256]{2,1,0:T(8,128)(2,1)S(1)} %collective-permute-done.13), channel_id=1, source_target_pairs={{0,15},{1,0},{2,1},{3,2},{4,3},{5,4},{6,5},{7,6},{8,7},{9,8},{10,9... | collective-permute-start | bytes 393224 | tf_op jit(solution)/shard_map/ppermute | solution.py:16
  162.3 6.7 %collective-permute-start.17 = (bf16[16,16,256]{2,1,0:T(8,128)(2,1)S(1)}, bf16[16,16,256]{2,1,0:T(8,128)(2,1)S(1)}, u32[]{:S(2)}, u32[]{:S(2)}) collective-permute-start(bf16[16,16,256]{2,1,0:T(8,128)(2,1)S(1)} %collective-permute-done.15), channel_id=1, source_target_pairs={{0,15},{1,0},{2,1},{3,2},{4,3},{5,4},{6,5},{7,6},{8,7},{9,8},{10,9... | collective-permute-start | bytes 393224 | tf_op jit(solution)/shard_map/ppermute | solution.py:16
  169.4 1.9 collective-permute-start.18
  171.4 6.7 %collective-permute-start.19 = (bf16[16,16,256]{2,1,0:T(8,128)(2,1)S(1)}, bf16[16,16,256]{2,1,0:T(8,128)(2,1)S(1)}, u32[]{:S(2)}, u32[]{:S(2)}) collective-permute-start(bf16[16,16,256]{2,1,0:T(8,128)(2,1)S(1)} %collective-permute-done.17), channel_id=1, source_target_pairs={{0,15},{1,0},{2,1},{3,2},{4,3},{5,4},{6,5},{7,6},{8,7},{9,8},{10,9... | collective-permute-start | bytes 393224 | tf_op jit(solution)/shard_map/ppermute | solution.py:16
  180.4 6.7 %collective-permute-start.21 = (bf16[16,16,256]{2,1,0:T(8,128)(2,1)S(1)}, bf16[16,16,256]{2,1,0:T(8,128)(2,1)S(1)}, u32[]{:S(2)}, u32[]{:S(2)}) collective-permute-start(bf16[16,16,256]{2,1,0:T(8,128)(2,1)S(1)} %collective-permute-done.19), channel_id=1, source_target_pairs={{0,15},{1,0},{2,1},{3,2},{4,3},{5,4},{6,5},{7,6},{8,7},{9,8},{10,9... | collective-permute-start | bytes 393224 | tf_op jit(solution)/shard_map/ppermute | solution.py:16
  189.4 6.7 %collective-permute-start.23 = (bf16[16,16,256]{2,1,0:T(8,128)(2,1)S(1)}, bf16[16,16,256]{2,1,0:T(8,128)(2,1)S(1)}, u32[]{:S(2)}, u32[]{:S(2)}) collective-permute-start(bf16[16,16,256]{2,1,0:T(8,128)(2,1)S(1)} %collective-permute-done.21), channel_id=1, source_target_pairs={{0,15},{1,0},{2,1},{3,2},{4,3},{5,4},{6,5},{7,6},{8,7},{9,8},{10,9... | collective-permute-start | bytes 393224 | tf_op jit(solution)/shard_map/ppermute | solution.py:16
  198.4 6.7 %collective-permute-start.25 = (bf16[16,16,256]{2,1,0:T(8,128)(2,1)S(1)}, bf16[16,16,256]{2,1,0:T(8,128)(2,1)S(1)}, u32[]{:S(2)}, u32[]{:S(2)}) collective-permute-start(bf16[16,16,256]{2,1,0:T(8,128)(2,1)S(1)} %collective-permute-done.23), channel_id=1, source_target_pairs={{0,15},{1,0},{2,1},{3,2},{4,3},{5,4},{6,5},{7,6},{8,7},{9,8},{10,9... | collective-permute-start | bytes 393224 | tf_op jit(solution)/shard_map/ppermute | solution.py:16
  207.5 7.1 %collective-permute-done.26 = bf16[16,16,256]{2,1,0:T(8,128)(2,1)S(1)} collective-permute-done((bf16[16,16,256]{2,1,0:T(8,128)(2,1)S(1)}, bf16[16,16,256]{2,1,0:T(8,128)(2,1)S(1)}, u32[]{:S(2)}, u32[]{:S(2)}) %collective-permute-start.26) | collective-permute-done | bytes 131104 | tf_op jit(solution)/shard_map/ppermute | solution.py:13
  218.2 65.0 %all-reduce.5.cloned.1.call-done = f32[16,16,256]{2,1,0:T(8,128)} async-done(((f32[16,16,256]{2,1,0:T(8,128)}), f32[16,16,256]{2,1,0:T(8,128)}) %all-reduce.5.cloned.1.call-update) | async-done | bytes 262160 | tf_op jit(solution)/shard_map/psum | solution.py:132
  (128 shorter events, 45.4 us)
Async XLA Ops:
  7.2 133.6 %reduce-scatter.2.cloned.1.call-start = ((), (), s32[]{:S(2)}) async-start(), calls=%async_computation.1 | async-start | bytes 786432 | tf_op jit(solution)/shard_map/reduce_scatter | solution.py:118
  8.3 20.6 %collective-permute-start.2 = (f32[16,1,256]{2,1,0:T(1,128)S(1)}, f32[16,1,256]{2,1,0:T(1,128)S(1)}, u32[]{:S(2)}, u32[]{:S(2)}) collective-permute-start(f32[16,1,256]{2,1,0:T(1,128)S(1)} %get-tuple-element.31), channel_id=1, source_target_pairs={{0,16},{16,32},{32,48},{48,64},{64,80},{80,96},{96,112},{112,128},... | collective-permute-start | bytes 49160 | tf_op jit(solution)/shard_map/ppermute | solution.py:31
  13.2 15.7 %collective-permute-start.3 = (f32[16,1,256]{2,1,0:T(1,128)S(1)}, f32[16,1,256]{2,1,0:T(1,128)S(1)}, u32[]{:S(2)}, u32[]{:S(2)}) collective-permute-start(f32[16,1,256]{2,1,0:T(1,128)S(1)} %get-tuple-element.32), channel_id=1, source_target_pairs={{16,0},{32,16},{48,32},{64,48},{80,64},{96,80},{112,96},{128,112},... | collective-permute-start | bytes 49160 | tf_op jit(solution)/shard_map/ppermute | solution.py:33
  19.5 20.1 %collective-permute-start = (f32[2,16,1,256]{3,2,1,0:T(1,128)S(1)}, f32[2,16,1,256]{3,2,1,0:T(1,128)S(1)}, u32[]{:S(2)}, u32[]{:S(2)}) collective-permute-start(f32[2,16,1,256]{3,2,1,0:T(1,128)S(1)} %get-tuple-element.21), channel_id=1, source_target_pairs={{16,0},{32,16},{48,32},{64,48},{80,64},{96,80},{112,96},{128,112},... | collective-permute-start | bytes 98312 | tf_op jit(solution)/shard_map/ppermute | solution.py:33
  21.4 18.1 %collective-permute-start.1 = (f32[2,16,1,256]{3,2,1,0:T(1,128)S(1)}, f32[2,16,1,256]{3,2,1,0:T(1,128)S(1)}, u32[]{:S(2)}, u32[]{:S(2)}) collective-permute-start(f32[2,16,1,256]{3,2,1,0:T(1,128)S(1)} %get-tuple-element.22), channel_id=1, source_target_pairs={{0,16},{16,32},{32,48},{48,64},{64,80},{80,96},{96,112},{112,128},... | collective-permute-start | bytes 98312 | tf_op jit(solution)/shard_map/ppermute | solution.py:31
  39.9 10.4 %collective-permute-start.6 = (f32[2,16,18,1]{3,2,1,0:T(8,128)S(1)}, f32[2,16,18,1]{3,2,1,0:T(8,128)S(1)}, u32[]{:S(2)}, u32[]{:S(2)}) collective-permute-start(f32[2,16,18,1]{3,2,1,0:T(8,128)S(1)} %get-tuple-element.16), channel_id=1, source_target_pairs={{0,1},{1,2},{2,3},{3,4},{4,5},{5,6},{6,7},{7,8},{8,9},{9,10},{10,1... | collective-permute-start | bytes 6920 | tf_op jit(solution)/shard_map/ppermute | solution.py:31
  42.1 12.0 %collective-permute-start.7 = (f32[2,16,18,1]{3,2,1,0:T(8,128)S(1)}, f32[2,16,18,1]{3,2,1,0:T(8,128)S(1)}, u32[]{:S(2)}, u32[]{:S(2)}) collective-permute-start(f32[2,16,18,1]{3,2,1,0:T(8,128)S(1)} %get-tuple-element.15), channel_id=1, source_target_pairs={{1,0},{2,1},{3,2},{4,3},{5,4},{6,5},{7,6},{8,7},{9,8},{10,9},{11,1... | collective-permute-start | bytes 6920 | tf_op jit(solution)/shard_map/ppermute | solution.py:33
  64.4 12.6 %collective-permute-start.10 = (f32[2,16,18,1]{3,2,1,0:T(8,128)S(1)}, f32[2,16,18,1]{3,2,1,0:T(8,128)S(1)}, u32[]{:S(2)}, u32[]{:S(2)}) collective-permute-start(f32[2,16,18,1]{3,2,1,0:T(8,128)S(1)} %get-tuple-element.13), channel_id=1, source_target_pairs={{1,0},{2,1},{3,2},{4,3},{5,4},{6,5},{7,6},{8,7},{9,8},{10,9},{11,1... | collective-permute-start | bytes 6920 | tf_op jit(solution)/shard_map/ppermute | solution.py:33
  65.7 13.0 %collective-permute-start.11 = (f32[2,16,18,1]{3,2,1,0:T(8,128)S(1)}, f32[2,16,18,1]{3,2,1,0:T(8,128)S(1)}, u32[]{:S(2)}, u32[]{:S(2)}) collective-permute-start(f32[2,16,18,1]{3,2,1,0:T(8,128)S(1)} %get-tuple-element.14), channel_id=1, source_target_pairs={{0,1},{1,2},{2,3},{3,4},{4,5},{5,6},{6,7},{7,8},{8,9},{9,10},{10,1... | collective-permute-start | bytes 6920 | tf_op jit(solution)/shard_map/ppermute | solution.py:31
  81.0 202.3 %all-reduce.5.cloned.1.call-start = ((), (), s32[]{:S(2)}) async-start(), calls=%async_computation.2 | async-start | bytes 524288 | tf_op jit(solution)/shard_map/psum | solution.py:132
  141.7 9.7 %collective-permute-start.12 = (bf16[16,16,256]{2,1,0:T(8,128)(2,1)S(1)}, bf16[16,16,256]{2,1,0:T(8,128)(2,1)S(1)}, u32[]{:S(2)}, u32[]{:S(2)}) collective-permute-start(bf16[16,16,256]{2,1,0:T(8,128)(2,1)S(1)} %get-tuple-element.8), channel_id=1, source_target_pairs={{0,1},{1,2},{2,3},{3,4},{4,5},{5,6},{6,7},{7,8},{8,9},{9,10},{10,1... | collective-permute-start | bytes 393224 | tf_op jit(solution)/shard_map/ppermute | solution.py:13
  151.4 9.0 %collective-permute-start.14 = (bf16[16,16,256]{2,1,0:T(8,128)(2,1)S(1)}, bf16[16,16,256]{2,1,0:T(8,128)(2,1)S(1)}, u32[]{:S(2)}, u32[]{:S(2)}) collective-permute-start(bf16[16,16,256]{2,1,0:T(8,128)(2,1)S(1)} %collective-permute-done.12), channel_id=1, source_target_pairs={{0,1},{1,2},{2,3},{3,4},{4,5},{5,6},{6,7},{7,8},{8,9},{9,10},{10,1... | collective-permute-start | bytes 393224 | tf_op jit(solution)/shard_map/ppermute | solution.py:13
  153.3 9.0 %collective-permute-start.15 = (bf16[16,16,256]{2,1,0:T(8,128)(2,1)S(1)}, bf16[16,16,256]{2,1,0:T(8,128)(2,1)S(1)}, u32[]{:S(2)}, u32[]{:S(2)}) collective-permute-start(bf16[16,16,256]{2,1,0:T(8,128)(2,1)S(1)} %collective-permute-done.13), channel_id=1, source_target_pairs={{0,15},{1,0},{2,1},{3,2},{4,3},{5,4},{6,5},{7,6},{8,7},{9,8},{10,9... | collective-permute-start | bytes 393224 | tf_op jit(solution)/shard_map/ppermute | solution.py:16
  160.4 9.0 %collective-permute-start.16 = (bf16[16,16,256]{2,1,0:T(8,128)(2,1)S(1)}, bf16[16,16,256]{2,1,0:T(8,128)(2,1)S(1)}, u32[]{:S(2)}, u32[]{:S(2)}) collective-permute-start(bf16[16,16,256]{2,1,0:T(8,128)(2,1)S(1)} %collective-permute-done.14), channel_id=1, source_target_pairs={{0,1},{1,2},{2,3},{3,4},{4,5},{5,6},{6,7},{7,8},{8,9},{9,10},{10,1... | collective-permute-start | bytes 393224 | tf_op jit(solution)/shard_map/ppermute | solution.py:13
  162.3 9.0 %collective-permute-start.17 = (bf16[16,16,256]{2,1,0:T(8,128)(2,1)S(1)}, bf16[16,16,256]{2,1,0:T(8,128)(2,1)S(1)}, u32[]{:S(2)}, u32[]{:S(2)}) collective-permute-start(bf16[16,16,256]{2,1,0:T(8,128)(2,1)S(1)} %collective-permute-done.15), channel_id=1, source_target_pairs={{0,15},{1,0},{2,1},{3,2},{4,3},{5,4},{6,5},{7,6},{8,7},{9,8},{10,9... | collective-permute-start | bytes 393224 | tf_op jit(solution)/shard_map/ppermute | solution.py:16
  169.4 9.0 %collective-permute-start.18 = (bf16[16,16,256]{2,1,0:T(8,128)(2,1)S(1)}, bf16[16,16,256]{2,1,0:T(8,128)(2,1)S(1)}, u32[]{:S(2)}, u32[]{:S(2)}) collective-permute-start(bf16[16,16,256]{2,1,0:T(8,128)(2,1)S(1)} %collective-permute-done.16), channel_id=1, source_target_pairs={{0,1},{1,2},{2,3},{3,4},{4,5},{5,6},{6,7},{7,8},{8,9},{9,10},{10,1... | collective-permute-start | bytes 393224 | tf_op jit(solution)/shard_map/ppermute | solution.py:13
  171.4 9.0 %collective-permute-start.19 = (bf16[16,16,256]{2,1,0:T(8,128)(2,1)S(1)}, bf16[16,16,256]{2,1,0:T(8,128)(2,1)S(1)}, u32[]{:S(2)}, u32[]{:S(2)}) collective-permute-start(bf16[16,16,256]{2,1,0:T(8,128)(2,1)S(1)} %collective-permute-done.17), channel_id=1, source_target_pairs={{0,15},{1,0},{2,1},{3,2},{4,3},{5,4},{6,5},{7,6},{8,7},{9,8},{10,9... | collective-permute-start | bytes 393224 | tf_op jit(solution)/shard_map/ppermute | solution.py:16
  178.4 9.0 %collective-permute-start.20 = (bf16[16,16,256]{2,1,0:T(8,128)(2,1)S(1)}, bf16[16,16,256]{2,1,0:T(8,128)(2,1)S(1)}, u32[]{:S(2)}, u32[]{:S(2)}) collective-permute-start(bf16[16,16,256]{2,1,0:T(8,128)(2,1)S(1)} %collective-permute-done.18), channel_id=1, source_target_pairs={{0,1},{1,2},{2,3},{3,4},{4,5},{5,6},{6,7},{7,8},{8,9},{9,10},{10,1... | collective-permute-start | bytes 393224 | tf_op jit(solution)/shard_map/ppermute | solution.py:13
  180.4 9.0 %collective-permute-start.21 = (bf16[16,16,256]{2,1,0:T(8,128)(2,1)S(1)}, bf16[16,16,256]{2,1,0:T(8,128)(2,1)S(1)}, u32[]{:S(2)}, u32[]{:S(2)}) collective-permute-start(bf16[16,16,256]{2,1,0:T(8,128)(2,1)S(1)} %collective-permute-done.19), channel_id=1, source_target_pairs={{0,15},{1,0},{2,1},{3,2},{4,3},{5,4},{6,5},{7,6},{8,7},{9,8},{10,9... | collective-permute-start | bytes 393224 | tf_op jit(solution)/shard_map/ppermute | solution.py:16
  187.5 9.0 %collective-permute-start.22 = (bf16[16,16,256]{2,1,0:T(8,128)(2,1)S(1)}, bf16[16,16,256]{2,1,0:T(8,128)(2,1)S(1)}, u32[]{:S(2)}, u32[]{:S(2)}) collective-permute-start(bf16[16,16,256]{2,1,0:T(8,128)(2,1)S(1)} %collective-permute-done.20), channel_id=1, source_target_pairs={{0,1},{1,2},{2,3},{3,4},{4,5},{5,6},{6,7},{7,8},{8,9},{9,10},{10,1... | collective-permute-start | bytes 393224 | tf_op jit(solution)/shard_map/ppermute | solution.py:13
  189.4 9.0 %collective-permute-start.23 = (bf16[16,16,256]{2,1,0:T(8,128)(2,1)S(1)}, bf16[16,16,256]{2,1,0:T(8,128)(2,1)S(1)}, u32[]{:S(2)}, u32[]{:S(2)}) collective-permute-start(bf16[16,16,256]{2,1,0:T(8,128)(2,1)S(1)} %collective-permute-done.21), channel_id=1, source_target_pairs={{0,15},{1,0},{2,1},{3,2},{4,3},{5,4},{6,5},{7,6},{8,7},{9,8},{10,9... | collective-permute-start | bytes 393224 | tf_op jit(solution)/shard_map/ppermute | solution.py:16
  196.5 9.0 %collective-permute-start.24 = (bf16[16,16,256]{2,1,0:T(8,128)(2,1)S(1)}, bf16[16,16,256]{2,1,0:T(8,128)(2,1)S(1)}, u32[]{:S(2)}, u32[]{:S(2)}) collective-permute-start(bf16[16,16,256]{2,1,0:T(8,128)(2,1)S(1)} %collective-permute-done.22), channel_id=1, source_target_pairs={{0,1},{1,2},{2,3},{3,4},{4,5},{5,6},{6,7},{7,8},{8,9},{9,10},{10,1... | collective-permute-start | bytes 393224 | tf_op jit(solution)/shard_map/ppermute | solution.py:13
  198.4 9.0 %collective-permute-start.25 = (bf16[16,16,256]{2,1,0:T(8,128)(2,1)S(1)}, bf16[16,16,256]{2,1,0:T(8,128)(2,1)S(1)}, u32[]{:S(2)}, u32[]{:S(2)}) collective-permute-start(bf16[16,16,256]{2,1,0:T(8,128)(2,1)S(1)} %collective-permute-done.23), channel_id=1, source_target_pairs={{0,15},{1,0},{2,1},{3,2},{4,3},{5,4},{6,5},{7,6},{8,7},{9,8},{10,9... | collective-permute-start | bytes 393224 | tf_op jit(solution)/shard_map/ppermute | solution.py:16
  205.5 9.1 %collective-permute-start.26 = (bf16[16,16,256]{2,1,0:T(8,128)(2,1)S(1)}, bf16[16,16,256]{2,1,0:T(8,128)(2,1)S(1)}, u32[]{:S(2)}, u32[]{:S(2)}) collective-permute-start(bf16[16,16,256]{2,1,0:T(8,128)(2,1)S(1)} %collective-permute-done.24), channel_id=1, source_target_pairs={{0,1},{1,2},{2,3},{3,4},{4,5},{5,6},{6,7},{7,8},{8,9},{9,10},{10,1... | collective-permute-start | bytes 393224 | tf_op jit(solution)/shard_map/ppermute | solution.py:13
  (24 other events, 421.9 us)
Sparse Core Ops, SparseCore 0:
  81.1 59.6 reduce-scatter.1
  217.2 65.9 all-reduce.4
